TPU v7x, 256 devices: a whole 4x4x8 slice. The times are simulated.
256 devices in a mesh: row: 64 (over z, y, core), col: 4 (over x).
Axes of the slice: x: 4, y: 4, z: 8, core: 2. Of those that a mesh axis runs over, the one named last changes fastest.
Arguments:
- train_points: float32 [16, 3, 64, 128], P(None, None, 'row'), may hold values from -6 to 6
- new_points: float32 [16, 256], replicated, may hold values from -6 to 6
- lengthscales: float32 [16], replicated, may hold values from 2.5 to 6
- factor: float32 [3, 64, 128, 3, 4, 2048], P(None, 'row', None, None, 'col'), may hold values from -0.02734375 to 0.02734375
- diag_inverse: float32 [3, 64, 128, 4, 2048], P(None, 'row', None, 'col'), may hold values from -3 to 3
Outputs:
- solution: float32 [3, 4, 64, 32, 256], P(None, 'col', 'row')
All inputs are finite; a program needn't handle non-finite values.
Results may differ from a plain program's by a relative error of at most 0.0001.
Values sent between devices are 32-bit elements; how exact they have to be, the bound alone decides.
No kernel may reach another device: no remote copies, remote signals or barrier semaphores. Data moves between devices by JAX's collectives and lax.ppermute only.
A program may use at most 128 MiB of HBM per device.

v0:
```python
import jax
import jax.numpy as jnp
from jax import lax
from jax.sharding import PartitionSpec as P


def on_device(train_points, new_points, lengthscales, factor, diag_inverse):
    highest = lax.Precision.HIGHEST
    panels = factor.shape[0]
    block_rows = factor.shape[2]
    quarter_cols = factor.shape[5]
    new_count = new_points.shape[1]
    share_rows = block_rows // lax.axis_size("col")
    scaled_train = (train_points / lengthscales[:, None, None, None]).reshape(
        train_points.shape[0], panels * block_rows
    )
    scaled_new = new_points / lengthscales[:, None]
    inner_products = jnp.dot(scaled_train.T, scaled_new, precision=highest)
    sqdist = (
        jnp.sum(scaled_train * scaled_train, axis=0)[:, None]
        + jnp.sum(scaled_new * scaled_new, axis=0)[None, :]
        - 2.0 * inner_products
    )
    kernel = jnp.exp(-0.5 * sqdist).reshape(panels, block_rows, new_count)
    factor_blocks = factor.reshape(panels, block_rows, panels, quarter_cols)
    inverse_blocks = diag_inverse.reshape(panels, block_rows, quarter_cols)
    panel_numbers = jnp.arange(panels)

    def update(partial_rows, panel, quarter, after):
        column_slab = lax.dynamic_index_in_dim(factor_blocks, panel, axis=2, keepdims=False)
        change = jnp.einsum("piq,qm->pim", column_slab, quarter, precision=highest)
        below = (panel_numbers > after)[:, None, None]
        return partial_rows + jnp.where(below, change, 0.0)

    def advance(panel, loop_state):
        partial_rows, solved, pending = loop_state
        own_partial = lax.dynamic_index_in_dim(partial_rows, panel, 0, keepdims=False)
        summed = lax.psum(own_partial, "col")
        residual = lax.dynamic_index_in_dim(kernel, panel, 0, keepdims=False) - summed
        inverse_block = lax.dynamic_index_in_dim(inverse_blocks, panel, 0, keepdims=False)
        product = jnp.einsum("iq,im->qm", inverse_block, residual, precision=highest)
        own_rows = lax.psum_scatter(product, "row", scatter_dimension=0, tiled=True)
        quarter = lax.all_gather(own_rows, "row", axis=0, tiled=True)
        solved = lax.dynamic_update_index_in_dim(solved, own_rows, panel, 0)
        partial_rows = update(partial_rows, panel, quarter, panel)
        return (partial_rows, solved, pending)

    initial = (
        jnp.zeros((panels, block_rows, new_count), jnp.float32),
        jnp.zeros((panels, share_rows, new_count), jnp.float32),
        jnp.zeros((quarter_cols, new_count), jnp.float32),
    )
    partial_rows, solved, pending = lax.fori_loop(0, panels, advance, initial)
    return solved.reshape(panels, 1, 1, share_rows, new_count)


def solution(mesh):
    return jax.shard_map(
        on_device,
        mesh=mesh,
        in_specs=(
            P(None, None, "row", None),
            P(),
            P(),
            P(None, "row", None, None, "col", None),
            P(None, "row", None, "col", None),
        ),
        out_specs=P(None, "col", "row", None, None),
        check_vma=False,
    )
```

profile of v0, /device:TPU:1, one launch (start us, length us, event | category | flops | bytes accessed | tf_op | source)
XLA Modules:
  0.0 868.2 jit_solution(1024487664733539460)
XLA Ops:
  6.5 0.9 fusion.27
  7.4 0.8 multiply_reduce_fusion.1
  8.3 2.0 fusion.24
  10.3 0.0 copy-start
  10.3 12.1 %copy.15 = f32[3,1,128,3,1,2048]{5,2,0,3,4,1:T(8,128)} copy(f32[3,1,128,3,1,2048]{5,4,3,2,1,0:T(1,128)} %param.10) | data formatting | bytes 18874368 | tf_op args[3]
  22.4 0.0 copy-done
  22.4 1.4 copy.16
  23.8 837.8 %while.16 = (s32[]{:T(128)}, f32[3,128,256]{2,1,0:T(8,128)}, f32[3,32,256]{2,1,0:T(8,128)}, f32[3,128,3,2048]{3,1,0,2:T(8,128)}, f32[3,128,2048]{2,1,0:T(8,128)S...) while((s32[]{:T(128)}, f32[3,128,256]{2,1,0:T(8,128)}, f32[3,32,256]{2,1,0:T(8,128)}, ...), condition=%wide.region_5.6_spmd.clone, body=%wide.region_2.5_spmd.clone.sunk | while | flops 3221585920 | bytes 24118516 | solution.py:53
  24.0 0.0 all-reduce.2.cloned.1.call-start
  24.1 0.7 dynamic-slice_bitcast_fusion.2
  24.8 0.0 all-reduce.2.cloned.1.call-update
  24.8 0.0 reduce-scatter.2.cloned.1.call-start
  24.9 50.3 %all-reduce.2.cloned.1.call-done = f32[128,256]{1,0:T(8,128)} async-done(((f32[128,256]{1,0:T(8,128)}), f32[128,256]{1,0:T(8,128)}) %all-reduce.2.cloned.1.call-update) | async-done | bytes 131088 | tf_op jit(solution)/shard_map/while/body/eval_jaxpr/psum | solution.py:38
  75.2 4.1 fusion.36
  79.3 0.0 reduce-scatter.2.cloned.1.call-update
  79.3 0.0 all-gather.2.cloned.1.call-start
  79.4 138.6 %reduce-scatter.2.cloned.1.call-done = f32[32,256]{1,0:T(8,128)} async-done(((f32[2048,256]{1,0:T(8,128)}), f32[32,256]{1,0:T(8,128)}) %reduce-scatter.2.cloned.1.call-update) | async-done | bytes 32784 | tf_op jit(solution)/shard_map/while/body/eval_jaxpr/reduce_scatter | solution.py:42
  218.0 0.0 all-gather.2.cloned.1.call-update
  218.1 1.4 bitcast_dynamic-update-slice_fusion.2
  219.4 82.4 %all-gather.2.cloned.1.call-done = f32[2048,256]{1,0:T(8,128)} async-done(((f32[32,256]{1,0:T(8,128)}), f32[2048,256]{1,0:T(8,128)}) %all-gather.2.cloned.1.call-update) | async-done | bytes 2097168 | tf_op jit(solution)/shard_map/while/body/eval_jaxpr/all_gather | solution.py:43
  301.9 6.0 fusion.37
  307.8 0.0 all-reduce.2.cloned.1.call-start
  307.8 1.0 broadcast_select_fusion.2
  308.9 0.7 dynamic-slice_bitcast_fusion.2
  309.5 0.0 all-reduce.2.cloned.1.call-update
  309.6 0.0 reduce-scatter.2.cloned.1.call-start
  309.6 42.5 %all-reduce.2.cloned.1.call-done = f32[128,256]{1,0:T(8,128)} async-done(((f32[128,256]{1,0:T(8,128)}), f32[128,256]{1,0:T(8,128)}) %all-reduce.2.cloned.1.call-update) | async-done | bytes 131088 | tf_op jit(solution)/shard_map/while/body/eval_jaxpr/psum | solution.py:38
  352.1 4.1 fusion.36
  356.2 0.0 reduce-scatter.2.cloned.1.call-update
  356.2 0.0 all-gather.2.cloned.1.call-start
  356.3 138.2 %reduce-scatter.2.cloned.1.call-done = f32[32,256]{1,0:T(8,128)} async-done(((f32[2048,256]{1,0:T(8,128)}), f32[32,256]{1,0:T(8,128)}) %reduce-scatter.2.cloned.1.call-update) | async-done | bytes 32784 | tf_op jit(solution)/shard_map/while/body/eval_jaxpr/reduce_scatter | solution.py:42
  494.5 0.0 all-gather.2.cloned.1.call-update
  494.5 1.4 bitcast_dynamic-update-slice_fusion.2
  495.9 82.6 %all-gather.2.cloned.1.call-done = f32[2048,256]{1,0:T(8,128)} async-done(((f32[32,256]{1,0:T(8,128)}), f32[2048,256]{1,0:T(8,128)}) %all-gather.2.cloned.1.call-update) | async-done | bytes 2097168 | tf_op jit(solution)/shard_map/while/body/eval_jaxpr/all_gather | solution.py:43
  578.5 6.0 fusion.37
  584.4 0.0 all-reduce.2.cloned.1.call-start
  584.5 1.0 broadcast_select_fusion.2
  585.5 0.7 dynamic-slice_bitcast_fusion.2
  586.1 0.0 all-reduce.2.cloned.1.call-update
  586.2 0.0 reduce-scatter.2.cloned.1.call-start
  586.2 42.8 %all-reduce.2.cloned.1.call-done = f32[128,256]{1,0:T(8,128)} async-done(((f32[128,256]{1,0:T(8,128)}), f32[128,256]{1,0:T(8,128)}) %all-reduce.2.cloned.1.call-update) | async-done | bytes 131088 | tf_op jit(solution)/shard_map/while/body/eval_jaxpr/psum | solution.py:38
  629.0 4.1 fusion.36
  633.2 0.0 reduce-scatter.2.cloned.1.call-update
  633.2 0.0 all-gather.2.cloned.1.call-start
  633.2 138.6 %reduce-scatter.2.cloned.1.call-done = f32[32,256]{1,0:T(8,128)} async-done(((f32[2048,256]{1,0:T(8,128)}), f32[32,256]{1,0:T(8,128)}) %reduce-scatter.2.cloned.1.call-update) | async-done | bytes 32784 | tf_op jit(solution)/shard_map/while/body/eval_jaxpr/reduce_scatter | solution.py:42
  771.9 0.0 all-gather.2.cloned.1.call-update
  771.9 1.4 bitcast_dynamic-update-slice_fusion.2
  773.3 82.4 %all-gather.2.cloned.1.call-done = f32[2048,256]{1,0:T(8,128)} async-done(((f32[32,256]{1,0:T(8,128)}), f32[2048,256]{1,0:T(8,128)}) %all-gather.2.cloned.1.call-update) | async-done | bytes 2097168 | tf_op jit(solution)/shard_map/while/body/eval_jaxpr/all_gather | solution.py:43
  855.7 6.0 fusion.37
  (6 shorter events, 0.1 us)
Async XLA Ops:
  10.3 12.1 %copy-start = (f32[3,1,128,1,2048]{4,3,2,1,0:T(1,128)S(1)}, f32[3,1,128,1,2048]{4,3,2,1,0:T(1,128)}, u32[]{:S(2)}) copy-start(f32[3,1,128,1,2048]{4,3,2,1,0:T(1,128)} %param.11) | copy-start | bytes 9437188
  24.0 51.2 %all-reduce.2.cloned.1.call-start = ((), (), s32[]{:S(2)}) async-start(), calls=%async_computation.1 | async-start | bytes 262144 | tf_op jit(solution)/shard_map/while/body/eval_jaxpr/psum | solution.py:38
  24.8 193.2 %reduce-scatter.2.cloned.1.call-start = ((), (), s32[]{:S(2)}) async-start(), calls=%async_computation.2 | async-start | bytes 2129920 | tf_op jit(solution)/shard_map/while/body/eval_jaxpr/reduce_scatter | solution.py:42
  79.3 222.5 %all-gather.2.cloned.1.call-start = ((), (), s32[]{:S(2)}) async-start(), calls=%async_computation.3 | async-start | bytes 2129920 | tf_op jit(solution)/shard_map/while/body/eval_jaxpr/all_gather | solution.py:43
  307.8 44.3 %all-reduce.2.cloned.1.call-start = ((), (), s32[]{:S(2)}) async-start(), calls=%async_computation.1 | async-start | bytes 262144 | tf_op jit(solution)/shard_map/while/body/eval_jaxpr/psum | solution.py:38
  309.6 184.9 %reduce-scatter.2.cloned.1.call-start = ((), (), s32[]{:S(2)}) async-start(), calls=%async_computation.2 | async-start | bytes 2129920 | tf_op jit(solution)/shard_map/while/body/eval_jaxpr/reduce_scatter | solution.py:42
  356.2 222.2 %all-gather.2.cloned.1.call-start = ((), (), s32[]{:S(2)}) async-start(), calls=%async_computation.3 | async-start | bytes 2129920 | tf_op jit(solution)/shard_map/while/body/eval_jaxpr/all_gather | solution.py:43
  584.4 44.6 %all-reduce.2.cloned.1.call-start = ((), (), s32[]{:S(2)}) async-start(), calls=%async_computation.1 | async-start | bytes 262144 | tf_op jit(solution)/shard_map/while/body/eval_jaxpr/psum | solution.py:38
  586.2 185.7 %reduce-scatter.2.cloned.1.call-start = ((), (), s32[]{:S(2)}) async-start(), calls=%async_computation.2 | async-start | bytes 2129920 | tf_op jit(solution)/shard_map/while/body/eval_jaxpr/reduce_scatter | solution.py:42
  633.2 222.5 %all-gather.2.cloned.1.call-start = ((), (), s32[]{:S(2)}) async-start(), calls=%async_computation.3 | async-start | bytes 2129920 | tf_op jit(solution)/shard_map/while/body/eval_jaxpr/all_gather | solution.py:43
Sparse Core Ops, SparseCore 0:
  27.2 47.9 all-reduce.1
  79.8 138.1 reduce-scatter.1
  220.8 81.0 all-gather.1
  310.7 41.4 all-reduce.1
  356.6 137.9 reduce-scatter.1
  497.1 81.3 all-gather.1
  587.6 41.4 all-reduce.1
  633.6 138.1 reduce-scatter.1
  774.6 81.0 all-gather.1
where the time goes:
time: 869 us; the launch traced here: 868 us
  waiting for transfers between devices  799 us (92%)
  matrix products  32.3 us (4%)
  local copies, waits for them, and re-layouts  19.7 us (2%)
  between operations  13.1 us (2%)
    reduce_scatter x3, waiting for transfers between devices, advance(): own_rows = lax.psum_scatter(product, 'row', scatter_dimension=0, tiled=True)  415 us
    all_gather x3, waiting for transfers between devices, advance(): quarter = lax.all_gather(own_rows, 'row', axis=0, tiled=True)  247 us
    psum x3, waiting for transfers between devices, advance(): summed = lax.psum(own_partial, 'col')  136 us
    dot_general x3, matrix products, update(): change = jnp.einsum('piq,qm->pim', column_slab, quarter, precision=highest)  17.9 us
  transfers between devices with their start and end apart: 9, of which 9 were waited for; matrix products, arithmetic and copies ran while one was open for 0% of the time, Pallas kernels for 0%

commit v1 on v0

--- a/solution.py
+++ b/solution.py
@@ -40,7 +40,9 @@
         inverse_block = lax.dynamic_index_in_dim(inverse_blocks, panel, 0, keepdims=False)
         product = jnp.einsum("iq,im->qm", inverse_block, residual, precision=highest)
         own_rows = lax.psum_scatter(product, "row", scatter_dimension=0, tiled=True)
-        quarter = lax.all_gather(own_rows, "row", axis=0, tiled=True)
+        quarter = jnp.concatenate(
+            lax.all_to_all(jnp.stack([own_rows] * lax.axis_size("row")), "row", 0, 0), axis=0
+        )
         solved = lax.dynamic_update_index_in_dim(solved, own_rows, panel, 0)
         partial_rows = update(partial_rows, panel, quarter, panel)
         return (partial_rows, solved, pending)

time: 869 us -> 812 us (0.934)
  waiting for transfers between devices: 799 us -> 700 us
  starting transfers between devices: 0.3 us -> 39.1 us
    all_gather x3 -> x0, waiting for transfers between devices: 247 us -> none  [advance(): quarter = lax.all_gather(own_rows, 'row', axis=0, tiled=True)]
    all_to_all x0 -> x3, waiting for transfers between devices: none -> 147 us  [advance(): lax.all_to_all(jnp.stack([own_rows] * lax.axis_size('row')), 'row', 0, 0)]
    all_to_all x0 -> x3, starting transfers between devices: none -> 38.9 us  [advance(): lax.all_to_all(jnp.stack([own_rows] * lax.axis_size('row')), 'row', 0, 0)]
where the time goes in v1:
time: 812 us; the launch traced here: 811 us
  waiting for transfers between devices  700 us (86%)
  starting transfers between devices  39.1 us (5%)
  matrix products  28.2 us (3%)
  local copies, waits for them, and re-layouts  28.1 us (3%)
  between operations  13.4 us (2%)
    reduce_scatter x3, waiting for transfers between devices, advance(): own_rows = lax.psum_scatter(product, 'row', scatter_dimension=0, tiled=True)  414 us
    all_to_all x3, waiting for transfers between devices, advance(): lax.all_to_all(jnp.stack([own_rows] * lax.axis_size('row')), 'row', 0, 0)  147 us
    psum x3, waiting for transfers between devices, advance(): summed = lax.psum(own_partial, 'col')  138 us
    all_to_all x3, starting transfers between devices, advance(): lax.all_to_all(jnp.stack([own_rows] * lax.axis_size('row')), 'row', 0, 0)  38.9 us
    unnamed x2, local copies, waits for them, and re-layouts  16.9 us
  transfers between devices with their start and end apart: 9, of which 9 were waited for; matrix products, arithmetic and copies ran while one was open for 0% of the time, Pallas kernels for 0%

profile of v1, /device:TPU:1, one launch (start us, length us, event | category | flops | bytes accessed | tf_op | source)
XLA Modules:
  0.0 810.9 jit_solution(12055433137899751203)
XLA Ops:
  6.5 0.8 multiply_reduce_fusion.1
  7.3 0.9 fusion.22
  8.3 1.3 fusion.19
  9.6 4.9 copy.16
  14.5 12.0 %copy.15 = f32[3,1,128,3,1,2048]{5,2,0,3,4,1:T(8,128)} copy(f32[3,1,128,3,1,2048]{5,4,3,2,1,0:T(1,128)} %param.10) | data formatting | bytes 18874368 | tf_op args[3]
  26.4 777.6 %while.16 = (s32[]{:T(128)}, f32[3,128,256]{2,1,0:T(8,128)S(1)}, f32[3,32,256]{2,1,0:T(8,128)}, f32[3,128,3,2048]{3,1,0,2:T(8,128)}, f32[3,128,2048]{2,1,0:T(8,1...) while((s32[]{:T(128)}, f32[3,128,256]{2,1,0:T(8,128)S(1)}, f32[3,32,256]{2,1,0:T(8,128)}, ...), condition=%wide.region_5.6_spmd.clone, body=%wide.region_2.5_spmd.clone.sunk | while | flops 3221585920 | bytes 26281224 | solution.py:55
  26.4 0.0 all-reduce.2.cloned.1.call-start
  26.5 0.7 dynamic-slice_bitcast_fusion.2
  27.2 0.0 all-reduce.2.cloned.1.call-update
  27.2 0.0 reduce-scatter.2.cloned.1.call-start
  27.2 50.4 %all-reduce.2.cloned.1.call-done = f32[128,256]{1,0:T(8,128)} async-done(((f32[128,256]{1,0:T(8,128)}), f32[128,256]{1,0:T(8,128)}) %all-reduce.2.cloned.1.call-update) | async-done | bytes 131088 | tf_op jit(solution)/shard_map/while/body/eval_jaxpr/psum | solution.py:38
  77.6 4.4 fusion.32
  82.0 0.0 reduce-scatter.2.cloned.1.call-update
  82.0 138.4 %reduce-scatter.2.cloned.1.call-done = f32[32,256]{1,0:T(8,128)} async-done(((f32[2048,256]{1,0:T(8,128)}), f32[32,256]{1,0:T(8,128)}) %reduce-scatter.2.cloned.1.call-update) | async-done | bytes 32784 | tf_op jit(solution)/shard_map/while/body/eval_jaxpr/reduce_scatter | solution.py:42
  220.4 0.0 copy-start
  220.4 2.4 stack.13
  222.9 12.7 %all-to-all-start = ((f32[64,32,256]{2,1,0:T(8,128)}), f32[64,32,256]{2,1,0:T(8,128)S(1)}, u32[]{:S(2)}, u32[]{:S(2)}) async-start(f32[64,32,256]{2,1,0:T(8,128)} %stack.13), calls=%async_computation.1 | async-start | bytes 4194304 | tf_op jit(solution)/shard_map/while/body/eval_jaxpr/all_to_all | solution.py:44
  235.6 0.0 copy-done
  235.6 0.6 bitcast_dynamic-update-slice_fusion.2
  236.2 49.0 %all-to-all-done = f32[64,32,256]{2,1,0:T(8,128)S(1)} async-done(((f32[64,32,256]{2,1,0:T(8,128)}), f32[64,32,256]{2,1,0:T(8,128)S(1)}, u32[]{:S(2)}, u32[]{:S(2)}) %all-to-all-start) | async-done | bytes 2097184 | tf_op jit(solution)/shard_map/while/body/eval_jaxpr/all_to_all | solution.py:44
  285.3 4.5 fusion.33
  289.8 0.0 all-reduce.2.cloned.1.call-start
  289.9 0.7 dynamic-slice_bitcast_fusion.2
  290.6 0.0 all-reduce.2.cloned.1.call-update
  290.6 0.0 reduce-scatter.2.cloned.1.call-start
  290.7 44.1 %all-reduce.2.cloned.1.call-done = f32[128,256]{1,0:T(8,128)} async-done(((f32[128,256]{1,0:T(8,128)}), f32[128,256]{1,0:T(8,128)}) %all-reduce.2.cloned.1.call-update) | async-done | bytes 131088 | tf_op jit(solution)/shard_map/while/body/eval_jaxpr/psum | solution.py:38
  334.8 4.4 fusion.32
  339.2 0.0 reduce-scatter.2.cloned.1.call-update
  339.3 138.1 %reduce-scatter.2.cloned.1.call-done = f32[32,256]{1,0:T(8,128)} async-done(((f32[2048,256]{1,0:T(8,128)}), f32[32,256]{1,0:T(8,128)}) %reduce-scatter.2.cloned.1.call-update) | async-done | bytes 32784 | tf_op jit(solution)/shard_map/while/body/eval_jaxpr/reduce_scatter | solution.py:42
  477.3 0.0 copy-start
  477.3 2.4 stack.13
  479.8 13.0 %all-to-all-start = ((f32[64,32,256]{2,1,0:T(8,128)}), f32[64,32,256]{2,1,0:T(8,128)S(1)}, u32[]{:S(2)}, u32[]{:S(2)}) async-start(f32[64,32,256]{2,1,0:T(8,128)} %stack.13), calls=%async_computation.1 | async-start | bytes 4194304 | tf_op jit(solution)/shard_map/while/body/eval_jaxpr/all_to_all | solution.py:44
  492.8 0.0 copy-done
  492.8 0.6 bitcast_dynamic-update-slice_fusion.2
  493.4 49.0 %all-to-all-done = f32[64,32,256]{2,1,0:T(8,128)S(1)} async-done(((f32[64,32,256]{2,1,0:T(8,128)}), f32[64,32,256]{2,1,0:T(8,128)S(1)}, u32[]{:S(2)}, u32[]{:S(2)}) %all-to-all-start) | async-done | bytes 2097184 | tf_op jit(solution)/shard_map/while/body/eval_jaxpr/all_to_all | solution.py:44
  542.5 4.5 fusion.33
  547.0 0.0 all-reduce.2.cloned.1.call-start
  547.1 0.7 dynamic-slice_bitcast_fusion.2
  547.8 0.0 all-reduce.2.cloned.1.call-update
  547.8 0.0 reduce-scatter.2.cloned.1.call-start
  547.9 43.8 %all-reduce.2.cloned.1.call-done = f32[128,256]{1,0:T(8,128)} async-done(((f32[128,256]{1,0:T(8,128)}), f32[128,256]{1,0:T(8,128)}) %all-reduce.2.cloned.1.call-update) | async-done | bytes 131088 | tf_op jit(solution)/shard_map/while/body/eval_jaxpr/psum | solution.py:38
  591.7 4.4 fusion.32
  596.1 0.0 reduce-scatter.2.cloned.1.call-update
  596.2 138.0 %reduce-scatter.2.cloned.1.call-done = f32[32,256]{1,0:T(8,128)} async-done(((f32[2048,256]{1,0:T(8,128)}), f32[32,256]{1,0:T(8,128)}) %reduce-scatter.2.cloned.1.call-update) | async-done | bytes 32784 | tf_op jit(solution)/shard_map/while/body/eval_jaxpr/reduce_scatter | solution.py:42
  734.2 0.0 copy-start
  734.2 2.4 stack.13
  736.7 13.1 %all-to-all-start = ((f32[64,32,256]{2,1,0:T(8,128)}), f32[64,32,256]{2,1,0:T(8,128)S(1)}, u32[]{:S(2)}, u32[]{:S(2)}) async-start(f32[64,32,256]{2,1,0:T(8,128)} %stack.13), calls=%async_computation.1 | async-start | bytes 4194304 | tf_op jit(solution)/shard_map/while/body/eval_jaxpr/all_to_all | solution.py:44
  749.8 0.0 copy-done
  749.8 0.6 bitcast_dynamic-update-slice_fusion.2
  750.4 49.0 %all-to-all-done = f32[64,32,256]{2,1,0:T(8,128)S(1)} async-done(((f32[64,32,256]{2,1,0:T(8,128)}), f32[64,32,256]{2,1,0:T(8,128)S(1)}, u32[]{:S(2)}, u32[]{:S(2)}) %all-to-all-start) | async-done | bytes 2097184 | tf_op jit(solution)/shard_map/while/body/eval_jaxpr/all_to_all | solution.py:44
  799.5 4.5 fusion.33
  (8 shorter events, 0.1 us)
Async XLA Ops:
  26.4 51.1 %all-reduce.2.cloned.1.call-start = ((), (), s32[]{:S(2)}) async-start(), calls=%async_computation.2 | async-start | bytes 262144 | tf_op jit(solution)/shard_map/while/body/eval_jaxpr/psum | solution.py:38
  27.2 193.2 %reduce-scatter.2.cloned.1.call-start = ((), (), s32[]{:S(2)}) async-start(), calls=%async_computation.3 | async-start | bytes 2129920 | tf_op jit(solution)/shard_map/while/body/eval_jaxpr/reduce_scatter | solution.py:42
  220.4 15.2 %copy-start = (f32[32,256]{1,0:T(8,128)S(1)}, f32[32,256]{1,0:T(8,128)}, u32[]{:S(2)}) copy-start(f32[32,256]{1,0:T(8,128)} %reduce-scatter.2.cloned.1.call-done) | copy-start | bytes 98308 | tf_op jit(solution)/shard_map/while
  222.9 62.4 %all-to-all-start = ((f32[64,32,256]{2,1,0:T(8,128)}), f32[64,32,256]{2,1,0:T(8,128)S(1)}, u32[]{:S(2)}, u32[]{:S(2)}) async-start(f32[64,32,256]{2,1,0:T(8,128)} %stack.13), calls=%async_computation.1 | async-start | bytes 4194304 | tf_op jit(solution)/shard_map/while/body/eval_jaxpr/all_to_all | solution.py:44
  289.8 45.0 %all-reduce.2.cloned.1.call-start = ((), (), s32[]{:S(2)}) async-start(), calls=%async_computation.2 | async-start | bytes 262144 | tf_op jit(solution)/shard_map/while/body/eval_jaxpr/psum | solution.py:38
  290.6 186.7 %reduce-scatter.2.cloned.1.call-start = ((), (), s32[]{:S(2)}) async-start(), calls=%async_computation.3 | async-start | bytes 2129920 | tf_op jit(solution)/shard_map/while/body/eval_jaxpr/reduce_scatter | solution.py:42
  477.3 15.5 %copy-start = (f32[32,256]{1,0:T(8,128)S(1)}, f32[32,256]{1,0:T(8,128)}, u32[]{:S(2)}) copy-start(f32[32,256]{1,0:T(8,128)} %reduce-scatter.2.cloned.1.call-done) | copy-start | bytes 98308 | tf_op jit(solution)/shard_map/while
  479.8 62.7 %all-to-all-start = ((f32[64,32,256]{2,1,0:T(8,128)}), f32[64,32,256]{2,1,0:T(8,128)S(1)}, u32[]{:S(2)}, u32[]{:S(2)}) async-start(f32[64,32,256]{2,1,0:T(8,128)} %stack.13), calls=%async_computation.1 | async-start | bytes 4194304 | tf_op jit(solution)/shard_map/while/body/eval_jaxpr/all_to_all | solution.py:44
  547.0 44.7 %all-reduce.2.cloned.1.call-start = ((), (), s32[]{:S(2)}) async-start(), calls=%async_computation.2 | async-start | bytes 262144 | tf_op jit(solution)/shard_map/while/body/eval_jaxpr/psum | solution.py:38
  547.8 186.4 %reduce-scatter.2.cloned.1.call-start = ((), (), s32[]{:S(2)}) async-start(), calls=%async_computation.3 | async-start | bytes 2129920 | tf_op jit(solution)/shard_map/while/body/eval_jaxpr/reduce_scatter | solution.py:42
  734.2 15.6 %copy-start = (f32[32,256]{1,0:T(8,128)S(1)}, f32[32,256]{1,0:T(8,128)}, u32[]{:S(2)}) copy-start(f32[32,256]{1,0:T(8,128)} %reduce-scatter.2.cloned.1.call-done) | copy-start | bytes 98308 | tf_op jit(solution)/shard_map/while
  736.7 62.8 %all-to-all-start = ((f32[64,32,256]{2,1,0:T(8,128)}), f32[64,32,256]{2,1,0:T(8,128)S(1)}, u32[]{:S(2)}, u32[]{:S(2)}) async-start(f32[64,32,256]{2,1,0:T(8,128)} %stack.13), calls=%async_computation.1 | async-start | bytes 4194304 | tf_op jit(solution)/shard_map/while/body/eval_jaxpr/all_to_all | solution.py:44
Sparse Core Ops, SparseCore 0:
  29.6 47.9 all-reduce.1
  82.2 138.1 reduce-scatter.1
  293.0 41.7 all-reduce.1
  339.4 137.9 reduce-scatter.1
  549.9 41.7 all-reduce.1
  596.3 137.8 reduce-scatter.1
